TPU v7x, 256 devices: a whole 4x4x8 slice. The times are simulated.
256 devices in a mesh: gx: 16 (over x, y), gy: 16 (over z, core).
Axes of the slice: x: 4, y: 4, z: 8, core: 2. Of those that a mesh axis runs over, the one named last changes fastest.
Arguments:
- permeability: float32 [1, 16, 128, 2048], P(None, None, 'gx', 'gy'), may hold values from 0.2 to 5
- saturation: float32 [1, 16, 128, 2048], P(None, None, 'gx', 'gy'), may hold values from 0.1 to 0.9
- pressure_old: float32 [1, 16, 128, 2048], P(None, None, 'gx', 'gy'), may hold values from -6 to 6
- source: float32 [16, 128, 2048], P(None, 'gx', 'gy'), may hold values from -25 to 25
Outputs:
- pressure: float32 [1, 16, 128, 2048], P(None, None, 'gx', 'gy')
- saturation_new: float32 [1, 16, 128, 2048], P(None, None, 'gx', 'gy')
All inputs are finite; a program needn't handle non-finite values.
Results may differ from a plain program's by a relative error of at most 0.0003.
Values sent between devices are 32-bit elements; how exact they have to be, the bound alone decides.
No kernel may reach another device: no remote copies, remote signals or barrier semaphores. Data moves between devices by JAX's collectives and lax.ppermute only.
A program may use at most 64 MiB of HBM per device.

v0:
```python
import jax
import jax.numpy as jnp
from jax import lax
from jax.sharding import PartitionSpec as P

ITERS = 2
storage_term = 0.5
vertical_ratio = 0.1
step_ratio = 0.05
water_viscosity = 1.0
oil_viscosity = 2.0


def padded_2(x, sides, width):
    for axis, dim in sides:
        size, length = (lax.axis_size(axis), x.shape[dim])
        up = [(i, (i + 1) % size) for i in range(size - 1)]
        down = [(j, i) for i, j in up]
        last = lax.slice_in_dim(x, length - width, length, axis=dim)
        first = lax.slice_in_dim(x, 0, width, axis=dim)
        before = lax.ppermute(last, axis, up)
        after = lax.ppermute(first, axis, down)
        x = jnp.concatenate([before, x, after], axis=dim)
    return x


def total_mobility(values):
    return values * values / water_viscosity + (1.0 - values) * (1.0 - values) / oil_viscosity


def water_fraction(values):
    return values * values / water_viscosity / total_mobility(values)


def coefficient(perm_left, perm_right, mobile_left, mobile_right, scaling):
    summed = perm_left + perm_right
    guarded = jnp.where(summed > 0.0, summed, 1.0)
    harmonic = jnp.where(summed > 0.0, 2.0 * perm_left * perm_right / guarded, 0.0)
    return scaling * harmonic * (0.5 * (mobile_left + mobile_right))


def across_pairs(padded, border, margin):
    rows_across = padded.shape[-2] - 2 * border
    rows_along = padded.shape[-1] - 2 * border
    block = padded[
        ...,
        border - margin - 1 : border + rows_across + margin + 1,
        border - margin : border + rows_along + margin,
    ]
    return (block[..., :-1, :], block[..., 1:, :])


def along_pairs(padded, border, margin):
    rows_across = padded.shape[-2] - 2 * border
    rows_along = padded.shape[-1] - 2 * border
    block = padded[
        ...,
        border - margin : border + rows_across + margin,
        border - margin - 1 : border + rows_along + margin + 1,
    ]
    return (block[..., :-1], block[..., 1:])


def interior(padded, border, margin):
    rows_across = padded.shape[-2] - 2 * border
    rows_along = padded.shape[-1] - 2 * border
    return padded[
        ...,
        border - margin : border + rows_across + margin,
        border - margin : border + rows_along + margin,
    ]


def vertical_pairs(values):
    widened = jnp.pad(values, ((0, 0), (1, 1), (0, 0), (0, 0)))
    return (widened[:, :-1], widened[:, 1:])


def face_terms(perm_wide, sat_wide, border, margin):
    mobile = total_mobility(sat_wide)
    perm_left, perm_right = across_pairs(perm_wide, border, margin)
    mobile_left, mobile_right = across_pairs(mobile, border, margin)
    across = coefficient(perm_left, perm_right, mobile_left, mobile_right, 1.0)
    perm_left, perm_right = along_pairs(perm_wide, border, margin)
    mobile_left, mobile_right = along_pairs(mobile, border, margin)
    along = coefficient(perm_left, perm_right, mobile_left, mobile_right, 1.0)
    perm_low, perm_high = vertical_pairs(interior(perm_wide, border, margin))
    mobile_low, mobile_high = vertical_pairs(interior(mobile, border, margin))
    vertical = coefficient(perm_low, perm_high, mobile_low, mobile_high, vertical_ratio)
    return (across, along, vertical)


def divergence(terms):
    across, along, vertical = terms
    return (
        vertical[:, 1:]
        - vertical[:, :-1]
        + (across[..., 1:, :] - across[..., :-1, :])
        + (along[..., 1:] - along[..., :-1])
    )


def diagonal_of(terms):
    across, along, vertical = terms
    return (
        storage_term
        + (vertical[:, 1:] + vertical[:, :-1])
        + (across[..., 1:, :] + across[..., :-1, :])
        + (along[..., 1:] + along[..., :-1])
    )


def fluxes(terms, pressure_wide, border, margin):
    across, along, vertical = terms
    left_side, right_side = across_pairs(pressure_wide, border, margin)
    flow_across = across * (left_side - right_side)
    left_side, right_side = along_pairs(pressure_wide, border, margin)
    flow_along = along * (left_side - right_side)
    lower_side, upper_side = vertical_pairs(interior(pressure_wide, border, margin))
    flow_vertical = vertical * (lower_side - upper_side)
    return (flow_across, flow_along, flow_vertical)


def apply_operator(terms, padded):
    return storage_term * interior(padded, 1, 0) + divergence(fluxes(terms, padded, 1, 0))


def transport(flows, sat_wide, border, margin, inflow_rate):
    fraction = water_fraction(sat_wide)
    flow_across, flow_along, flow_vertical = flows
    left_side, right_side = across_pairs(fraction, border, margin)
    water_across = flow_across * jnp.where(flow_across > 0.0, left_side, right_side)
    left_side, right_side = along_pairs(fraction, border, margin)
    water_along = flow_along * jnp.where(flow_along > 0.0, left_side, right_side)
    middle = interior(fraction, border, margin)
    lower_side, upper_side = vertical_pairs(middle)
    water_vertical = flow_vertical * jnp.where(flow_vertical > 0.0, lower_side, upper_side)
    current = interior(sat_wide, border, margin)
    gained = jnp.maximum(inflow_rate, 0.0) + jnp.minimum(inflow_rate, 0.0) * middle
    return current + step_ratio * (gained - divergence((water_across, water_along, water_vertical)))


def search_image(terms, values):
    padded = padded_2(values, (("gx", 2), ("gy", 3)), 1)
    return (apply_operator(terms, padded), padded)


def local_dot(former, latter):
    return jnp.sum(former * latter, axis=(1, 2, 3))


def per_sample(scalars):
    return scalars[:, None, None, None]


def energy(residual, precond):
    return lax.psum(local_dot(residual, precond), ("gx", "gy"))


def local(permeability, saturation, pressure_old, source):
    samples = permeability.shape[0]
    inflow_rate = source[None]
    stacked = jnp.concatenate([permeability, saturation, pressure_old], axis=0)
    padded = padded_2(stacked, (("gx", 2), ("gy", 3)), 1)
    border = 1
    perm_wide = padded[:samples]
    sat_wide = padded[samples : 2 * samples]
    old_wide = padded[2 * samples : 3 * samples]
    wide_terms = face_terms(perm_wide, sat_wide, border, border - 1)
    diagonal = diagonal_of(wide_terms)
    right_side = inflow_rate + storage_term * pressure_old
    solution = pressure_old
    residual = right_side - apply_operator(wide_terms, old_wide)
    precond = residual / diagonal
    direction = precond
    energy_now = energy(residual, precond)
    for sweep in range(ITERS):
        image_field, direction_wide = search_image(wide_terms, direction)
        curvature = lax.psum(local_dot(direction, image_field), ("gx", "gy"))
        step_size = energy_now / curvature
        solution = solution + per_sample(step_size) * direction
        if sweep + 1 < ITERS:
            residual = residual - per_sample(step_size) * image_field
            precond = residual / diagonal
            energy_next = energy(residual, precond)
            direction = precond + per_sample(energy_next / energy_now) * direction
            energy_now = energy_next
    pressure_wide = padded_2(solution, (("gx", 2), ("gy", 3)), 1)
    flows = fluxes(wide_terms, pressure_wide, 1, 0)
    first = transport(flows, sat_wide, 1, 0, inflow_rate)
    first_wide = padded_2(first, (("gx", 2), ("gy", 3)), 1)
    second = transport(flows, first_wide, 1, 0, inflow_rate)
    return (solution, second)


def solution(mesh):
    in_specs = (
        P(None, None, "gx", "gy"),
        P(None, None, "gx", "gy"),
        P(None, None, "gx", "gy"),
        P(None, "gx", "gy"),
    )
    out_specs = (P(None, None, "gx", "gy"), P(None, None, "gx", "gy"))
    return jax.shard_map(local, mesh=mesh, in_specs=in_specs, out_specs=out_specs, check_vma=False)
```

profile of v0, /device:TPU:121, one launch (start us, length us, event | category | flops | bytes accessed | tf_op | source)
XLA Modules:
  0.0 343.5 jit_solution(17763078292054774674)
XLA Ops:
  0.6 0.9 constant_dynamic-update-slice_fusion.2
  1.5 0.8 copy-done.1
  2.4 2.8 collective-permute-start
  5.2 2.5 collective-permute-start.1
  7.7 4.2 %collective-permute-done.1 = f32[3,16,1,128]{3,2,1,0:T(1,128)S(1)} collective-permute-done((f32[3,16,1,128]{3,2,1,0:T(1,128)S(1)}, f32[3,16,1,128]{3,2,1,0:T(1,128)S(1)}, u32[]{:S(2)}, u32[]{:S(2)}) %collective-permute-start.1) | collective-permute-done | bytes 24608 | tf_op jit(solution)/shard_map/ppermute | solution.py:22
  11.9 0.2 fusion.76
  12.1 6.7 %collective-permute-start.2 = (f32[3,16,10,1]{3,2,1,0:T(8,128)S(1)}, f32[3,16,10,1]{3,2,1,0:T(8,128)S(1)}, u32[]{:S(2)}, u32[]{:S(2)}) collective-permute-start(f32[3,16,10,1]{3,2,1,0:T(8,128)S(1)} %get-tuple-element.20), channel_id=1, source_target_pairs={{0,1},{1,2},{2,3},{3,4},{4,5},{5,6},{6,7},{7,8},{8,9},{9,10},{10,1... | collective-permute-start | bytes 5768 | tf_op jit(solution)/shard_map/ppermute | solution.py:21
  18.9 1.9 collective-permute-start.3
  20.8 2.8 collective-permute-done.2
  23.6 5.6 %collective-permute-done.3 = f32[3,16,10,1]{3,2,1,0:T(8,128)S(1)} collective-permute-done((f32[3,16,10,1]{3,2,1,0:T(8,128)S(1)}, f32[3,16,10,1]{3,2,1,0:T(8,128)S(1)}, u32[]{:S(2)}, u32[]{:S(2)}) %collective-permute-start.3) | collective-permute-done | bytes 1952 | tf_op jit(solution)/shard_map/ppermute | solution.py:22
  29.2 0.2 multiply_divide_fusion
  29.6 0.7 copy-done.4
  30.4 0.2 fusion.15
  30.8 0.7 copy-done.2
  31.6 1.9 collective-permute-start.4
  33.5 3.4 collective-permute-start.5
  37.0 3.0 collective-permute-done.5
  40.2 2.9 collective-permute-start.6
  43.1 1.9 collective-permute-start.7
  45.1 5.5 %collective-permute-done.7 = f32[1,16,10,1]{3,2,1,0:T(8,128)S(1)} collective-permute-done((f32[1,16,10,1]{3,2,1,0:T(8,128)S(1)}, f32[1,16,10,1]{3,2,1,0:T(8,128)S(1)}, u32[]{:S(2)}, u32[]{:S(2)}) %collective-permute-start.7) | collective-permute-done | bytes 672 | tf_op jit(solution)/shard_map/ppermute | solution.py:22
  50.7 0.7 multiply_reduce_fusion.1
  51.4 72.2 %all-reduce.8 = (f32[1]{0:T(128)}, f32[1]{0:T(128)}) all-reduce(f32[1]{0:T(128)} %bitcast.1, f32[1]{0:T(128)} %bitcast.2), channel_id=1, replica_groups=mesh['gx'=16,'gy'=16] {'gx','gy'}, use_global_device_ids=true, to_apply=%region_1.2 | all-reduce | flops 2 | bytes 16 | tf_op jit(solution)/shard_map/psum | solution.py:157
  125.0 0.7 multiply_reduce_fusion
  125.6 75.4 %psum.30 = f32[1]{0:T(128)} all-reduce(f32[1]{0:T(128)} %bitcast.4), channel_id=1, replica_groups=mesh['gx'=16,'gy'=16] {'gx','gy'}, use_global_device_ids=true, to_apply=%region_5.6 | all-reduce | flops 1 | bytes 8 | tf_op jit(solution)/shard_map/psum | solution.py:157
  202.4 3.1 collective-permute-start.8
  205.5 2.2 collective-permute-start.9
  207.7 4.3 %collective-permute-done.9 = f32[1,16,1,128]{3,2,1,0:T(1,128)S(1)} collective-permute-done((f32[1,16,1,128]{3,2,1,0:T(1,128)S(1)}, f32[1,16,1,128]{3,2,1,0:T(1,128)S(1)}, u32[]{:S(2)}, u32[]{:S(2)}) %collective-permute-start.9) | collective-permute-done | bytes 8224 | tf_op jit(solution)/shard_map/ppermute | solution.py:22
  212.1 4.8 %collective-permute-start.10 = (f32[1,16,10,1]{3,2,1,0:T(8,128)S(1)}, f32[1,16,10,1]{3,2,1,0:T(8,128)S(1)}, u32[]{:S(2)}, u32[]{:S(2)}) collective-permute-start(f32[1,16,10,1]{3,2,1,0:T(8,128)S(1)} %get-tuple-element.28), channel_id=1, source_target_pairs={{0,1},{1,2},{2,3},{3,4},{4,5},{5,6},{6,7},{7,8},{8,9},{9,10},{10,1... | collective-permute-start | bytes 1928 | tf_op jit(solution)/shard_map/ppermute | solution.py:21
  216.9 1.9 collective-permute-start.11
  218.9 5.5 %collective-permute-done.11 = f32[1,16,10,1]{3,2,1,0:T(8,128)S(1)} collective-permute-done((f32[1,16,10,1]{3,2,1,0:T(8,128)S(1)}, f32[1,16,10,1]{3,2,1,0:T(8,128)S(1)}, u32[]{:S(2)}, u32[]{:S(2)}) %collective-permute-start.11) | collective-permute-done | bytes 672 | tf_op jit(solution)/shard_map/ppermute | solution.py:22
  224.6 0.7 fusion.53
  225.3 72.9 %psum.31 = f32[1]{0:T(128)} all-reduce(f32[1]{0:T(128)} %bitcast.6), channel_id=1, replica_groups=mesh['gx'=16,'gy'=16] {'gx','gy'}, use_global_device_ids=true, to_apply=%region_7.8 | all-reduce | flops 1 | bytes 8 | tf_op jit(solution)/shard_map/psum | solution.py:179
  299.6 3.1 collective-permute-start.12
  302.7 2.2 collective-permute-start.13
  304.9 4.3 %collective-permute-done.13 = f32[1,16,1,128]{3,2,1,0:T(1,128)S(1)} collective-permute-done((f32[1,16,1,128]{3,2,1,0:T(1,128)S(1)}, f32[1,16,1,128]{3,2,1,0:T(1,128)S(1)}, u32[]{:S(2)}, u32[]{:S(2)}) %collective-permute-start.13) | collective-permute-done | bytes 8224 | tf_op jit(solution)/shard_map/ppermute | solution.py:22
  309.3 6.0 %collective-permute-start.14 = (f32[1,16,10,1]{3,2,1,0:T(8,128)S(1)}, f32[1,16,10,1]{3,2,1,0:T(8,128)S(1)}, u32[]{:S(2)}, u32[]{:S(2)}) collective-permute-start(f32[1,16,10,1]{3,2,1,0:T(8,128)S(1)} %get-tuple-element.26), channel_id=1, source_target_pairs={{0,1},{1,2},{2,3},{3,4},{4,5},{5,6},{6,7},{7,8},{8,9},{9,10},{10,1... | collective-permute-start | bytes 1928 | tf_op jit(solution)/shard_map/ppermute | solution.py:21
  315.3 1.9 collective-permute-start.15
  317.2 0.1 fusion.9
  317.4 5.4 %collective-permute-done.15 = f32[1,16,10,1]{3,2,1,0:T(8,128)S(1)} collective-permute-done((f32[1,16,10,1]{3,2,1,0:T(8,128)S(1)}, f32[1,16,10,1]{3,2,1,0:T(8,128)S(1)}, u32[]{:S(2)}, u32[]{:S(2)}) %collective-permute-start.15) | collective-permute-done | bytes 672 | tf_op jit(solution)/shard_map/ppermute | solution.py:22
  322.8 0.2 fusion.6
  323.1 1.9 collective-permute-start.16
  325.1 3.4 collective-permute-start.17
  328.4 3.1 collective-permute-done.17
  331.7 2.9 collective-permute-start.18
  334.6 1.9 collective-permute-start.19
  336.6 5.6 %collective-permute-done.19 = f32[1,16,10,1]{3,2,1,0:T(8,128)S(1)} collective-permute-done((f32[1,16,10,1]{3,2,1,0:T(8,128)S(1)}, f32[1,16,10,1]{3,2,1,0:T(8,128)S(1)}, u32[]{:S(2)}, u32[]{:S(2)}) %collective-permute-start.19) | collective-permute-done | bytes 672 | tf_op jit(solution)/shard_map/ppermute | solution.py:22
  342.1 0.2 add_divide_fusion
  342.8 0.8 fusion.43
  (52 shorter events, 2.1 us)
Async XLA Ops:
  0.6 0.9 copy-start.3
  1.5 0.8 copy-start.1
  2.4 5.3 %collective-permute-start = (f32[3,16,1,128]{3,2,1,0:T(1,128)S(1)}, f32[3,16,1,128]{3,2,1,0:T(1,128)S(1)}, u32[]{:S(2)}, u32[]{:S(2)}) collective-permute-start(f32[3,16,1,128]{3,2,1,0:T(1,128)S(1)} %get-tuple-element.22), channel_id=1, source_target_pairs={{0,16},{16,32},{32,48},{48,64},{64,80},{80,96},{96,112},{112,128},... | collective-permute-start | bytes 73736 | tf_op jit(solution)/shard_map/ppermute | solution.py:21
  5.2 6.7 %collective-permute-start.1 = (f32[3,16,1,128]{3,2,1,0:T(1,128)S(1)}, f32[3,16,1,128]{3,2,1,0:T(1,128)S(1)}, u32[]{:S(2)}, u32[]{:S(2)}) collective-permute-start(f32[3,16,1,128]{3,2,1,0:T(1,128)S(1)} %get-tuple-element.23), channel_id=1, source_target_pairs={{16,0},{32,16},{48,32},{64,48},{80,64},{96,80},{112,96},{128,112},... | collective-permute-start | bytes 73736 | tf_op jit(solution)/shard_map/ppermute | solution.py:22
  12.1 11.5 %collective-permute-start.2 = (f32[3,16,10,1]{3,2,1,0:T(8,128)S(1)}, f32[3,16,10,1]{3,2,1,0:T(8,128)S(1)}, u32[]{:S(2)}, u32[]{:S(2)}) collective-permute-start(f32[3,16,10,1]{3,2,1,0:T(8,128)S(1)} %get-tuple-element.20), channel_id=1, source_target_pairs={{0,1},{1,2},{2,3},{3,4},{4,5},{5,6},{6,7},{7,8},{8,9},{9,10},{10,1... | collective-permute-start | bytes 5768 | tf_op jit(solution)/shard_map/ppermute | solution.py:21
  18.9 10.3 %collective-permute-start.3 = (f32[3,16,10,1]{3,2,1,0:T(8,128)S(1)}, f32[3,16,10,1]{3,2,1,0:T(8,128)S(1)}, u32[]{:S(2)}, u32[]{:S(2)}) collective-permute-start(f32[3,16,10,1]{3,2,1,0:T(8,128)S(1)} %get-tuple-element.21), channel_id=1, source_target_pairs={{1,0},{2,1},{3,2},{4,3},{5,4},{6,5},{7,6},{8,7},{9,8},{10,9},{11,1... | collective-permute-start | bytes 5768 | tf_op jit(solution)/shard_map/ppermute | solution.py:22
  29.5 0.8 copy-start.4
  30.6 0.8 copy-start.2
  31.6 5.4 %collective-permute-start.4 = (f32[1,16,1,128]{3,2,1,0:T(1,128)S(1)}, f32[1,16,1,128]{3,2,1,0:T(1,128)S(1)}, u32[]{:S(2)}, u32[]{:S(2)}) collective-permute-start(f32[1,16,1,128]{3,2,1,0:T(1,128)S(1)} %get-tuple-element.38), channel_id=1, source_target_pairs={{0,16},{16,32},{32,48},{48,64},{64,80},{80,96},{96,112},{112,128},... | collective-permute-start | bytes 24584 | tf_op jit(solution)/shard_map/ppermute | solution.py:21
  33.5 6.5 %collective-permute-start.5 = (f32[1,16,1,128]{3,2,1,0:T(1,128)S(1)}, f32[1,16,1,128]{3,2,1,0:T(1,128)S(1)}, u32[]{:S(2)}, u32[]{:S(2)}) collective-permute-start(f32[1,16,1,128]{3,2,1,0:T(1,128)S(1)} %get-tuple-element.39), channel_id=1, source_target_pairs={{16,0},{32,16},{48,32},{64,48},{80,64},{96,80},{112,96},{128,112},... | collective-permute-start | bytes 24584 | tf_op jit(solution)/shard_map/ppermute | solution.py:22
  40.2 4.9 %collective-permute-start.6 = (f32[1,16,10,1]{3,2,1,0:T(8,128)S(1)}, f32[1,16,10,1]{3,2,1,0:T(8,128)S(1)}, u32[]{:S(2)}, u32[]{:S(2)}) collective-permute-start(f32[1,16,10,1]{3,2,1,0:T(8,128)S(1)} %get-tuple-element.30), channel_id=1, source_target_pairs={{0,1},{1,2},{2,3},{3,4},{4,5},{5,6},{6,7},{7,8},{8,9},{9,10},{10,1... | collective-permute-start | bytes 1928 | tf_op jit(solution)/shard_map/ppermute | solution.py:21
  43.1 7.5 %collective-permute-start.7 = (f32[1,16,10,1]{3,2,1,0:T(8,128)S(1)}, f32[1,16,10,1]{3,2,1,0:T(8,128)S(1)}, u32[]{:S(2)}, u32[]{:S(2)}) collective-permute-start(f32[1,16,10,1]{3,2,1,0:T(8,128)S(1)} %get-tuple-element.31), channel_id=1, source_target_pairs={{1,0},{2,1},{3,2},{4,3},{5,4},{6,5},{7,6},{8,7},{9,8},{10,9},{11,1... | collective-permute-start | bytes 1928 | tf_op jit(solution)/shard_map/ppermute | solution.py:22
  202.4 5.3 %collective-permute-start.8 = (f32[1,16,1,128]{3,2,1,0:T(1,128)S(1)}, f32[1,16,1,128]{3,2,1,0:T(1,128)S(1)}, u32[]{:S(2)}, u32[]{:S(2)}) collective-permute-start(f32[1,16,1,128]{3,2,1,0:T(1,128)S(1)} %get-tuple-element.36), channel_id=1, source_target_pairs={{0,16},{16,32},{32,48},{48,64},{64,80},{80,96},{96,112},{112,128},... | collective-permute-start | bytes 24584 | tf_op jit(solution)/shard_map/ppermute | solution.py:21
  205.5 6.5 %collective-permute-start.9 = (f32[1,16,1,128]{3,2,1,0:T(1,128)S(1)}, f32[1,16,1,128]{3,2,1,0:T(1,128)S(1)}, u32[]{:S(2)}, u32[]{:S(2)}) collective-permute-start(f32[1,16,1,128]{3,2,1,0:T(1,128)S(1)} %get-tuple-element.37), channel_id=1, source_target_pairs={{16,0},{32,16},{48,32},{64,48},{80,64},{96,80},{112,96},{128,112},... | collective-permute-start | bytes 24584 | tf_op jit(solution)/shard_map/ppermute | solution.py:22
  212.1 6.8 %collective-permute-start.10 = (f32[1,16,10,1]{3,2,1,0:T(8,128)S(1)}, f32[1,16,10,1]{3,2,1,0:T(8,128)S(1)}, u32[]{:S(2)}, u32[]{:S(2)}) collective-permute-start(f32[1,16,10,1]{3,2,1,0:T(8,128)S(1)} %get-tuple-element.28), channel_id=1, source_target_pairs={{0,1},{1,2},{2,3},{3,4},{4,5},{5,6},{6,7},{7,8},{8,9},{9,10},{10,1... | collective-permute-start | bytes 1928 | tf_op jit(solution)/shard_map/ppermute | solution.py:21
  216.9 7.5 %collective-permute-start.11 = (f32[1,16,10,1]{3,2,1,0:T(8,128)S(1)}, f32[1,16,10,1]{3,2,1,0:T(8,128)S(1)}, u32[]{:S(2)}, u32[]{:S(2)}) collective-permute-start(f32[1,16,10,1]{3,2,1,0:T(8,128)S(1)} %get-tuple-element.29), channel_id=1, source_target_pairs={{1,0},{2,1},{3,2},{4,3},{5,4},{6,5},{7,6},{8,7},{9,8},{10,9},{11,1... | collective-permute-start | bytes 1928 | tf_op jit(solution)/shard_map/ppermute | solution.py:22
  299.5 43.1 %copy-start = (f32[1,16,8,128]{3,2,1,0:T(8,128)}, f32[1,16,8,128]{3,2,1,0:T(8,128)S(1)}, u32[]{:S(2)}) copy-start(f32[1,16,8,128]{3,2,1,0:T(8,128)S(1)} %multiply_add_fusion.1) | copy-start | bytes 196612
  299.6 5.3 %collective-permute-start.12 = (f32[1,16,1,128]{3,2,1,0:T(1,128)S(1)}, f32[1,16,1,128]{3,2,1,0:T(1,128)S(1)}, u32[]{:S(2)}, u32[]{:S(2)}) collective-permute-start(f32[1,16,1,128]{3,2,1,0:T(1,128)S(1)} %get-tuple-element.34), channel_id=1, source_target_pairs={{0,16},{16,32},{32,48},{48,64},{64,80},{80,96},{96,112},{112,128},... | collective-permute-start | bytes 24584 | tf_op jit(solution)/shard_map/ppermute | solution.py:21
  302.7 6.5 %collective-permute-start.13 = (f32[1,16,1,128]{3,2,1,0:T(1,128)S(1)}, f32[1,16,1,128]{3,2,1,0:T(1,128)S(1)}, u32[]{:S(2)}, u32[]{:S(2)}) collective-permute-start(f32[1,16,1,128]{3,2,1,0:T(1,128)S(1)} %get-tuple-element.35), channel_id=1, source_target_pairs={{16,0},{32,16},{48,32},{64,48},{80,64},{96,80},{112,96},{128,112},... | collective-permute-start | bytes 24584 | tf_op jit(solution)/shard_map/ppermute | solution.py:22
  309.3 8.1 %collective-permute-start.14 = (f32[1,16,10,1]{3,2,1,0:T(8,128)S(1)}, f32[1,16,10,1]{3,2,1,0:T(8,128)S(1)}, u32[]{:S(2)}, u32[]{:S(2)}) collective-permute-start(f32[1,16,10,1]{3,2,1,0:T(8,128)S(1)} %get-tuple-element.26), channel_id=1, source_target_pairs={{0,1},{1,2},{2,3},{3,4},{4,5},{5,6},{6,7},{7,8},{8,9},{9,10},{10,1... | collective-permute-start | bytes 1928 | tf_op jit(solution)/shard_map/ppermute | solution.py:21
  315.3 7.5 %collective-permute-start.15 = (f32[1,16,10,1]{3,2,1,0:T(8,128)S(1)}, f32[1,16,10,1]{3,2,1,0:T(8,128)S(1)}, u32[]{:S(2)}, u32[]{:S(2)}) collective-permute-start(f32[1,16,10,1]{3,2,1,0:T(8,128)S(1)} %get-tuple-element.27), channel_id=1, source_target_pairs={{1,0},{2,1},{3,2},{4,3},{5,4},{6,5},{7,6},{8,7},{9,8},{10,9},{11,1... | collective-permute-start | bytes 1928 | tf_op jit(solution)/shard_map/ppermute | solution.py:22
  323.1 5.3 %collective-permute-start.16 = (f32[1,16,1,128]{3,2,1,0:T(1,128)S(1)}, f32[1,16,1,128]{3,2,1,0:T(1,128)S(1)}, u32[]{:S(2)}, u32[]{:S(2)}) collective-permute-start(f32[1,16,1,128]{3,2,1,0:T(1,128)S(1)} %get-tuple-element.32), channel_id=1, source_target_pairs={{0,16},{16,32},{32,48},{48,64},{64,80},{80,96},{96,112},{112,128},... | collective-permute-start | bytes 24584 | tf_op jit(solution)/shard_map/ppermute | solution.py:21
  325.1 6.5 %collective-permute-start.17 = (f32[1,16,1,128]{3,2,1,0:T(1,128)S(1)}, f32[1,16,1,128]{3,2,1,0:T(1,128)S(1)}, u32[]{:S(2)}, u32[]{:S(2)}) collective-permute-start(f32[1,16,1,128]{3,2,1,0:T(1,128)S(1)} %get-tuple-element.33), channel_id=1, source_target_pairs={{16,0},{32,16},{48,32},{64,48},{80,64},{96,80},{112,96},{128,112},... | collective-permute-start | bytes 24584 | tf_op jit(solution)/shard_map/ppermute | solution.py:22
  331.7 4.9 %collective-permute-start.18 = (f32[1,16,10,1]{3,2,1,0:T(8,128)S(1)}, f32[1,16,10,1]{3,2,1,0:T(8,128)S(1)}, u32[]{:S(2)}, u32[]{:S(2)}) collective-permute-start(f32[1,16,10,1]{3,2,1,0:T(8,128)S(1)} %get-tuple-element.24), channel_id=1, source_target_pairs={{0,1},{1,2},{2,3},{3,4},{4,5},{5,6},{6,7},{7,8},{8,9},{9,10},{10,1... | collective-permute-start | bytes 1928 | tf_op jit(solution)/shard_map/ppermute | solution.py:21
  334.6 7.5 %collective-permute-start.19 = (f32[1,16,10,1]{3,2,1,0:T(8,128)S(1)}, f32[1,16,10,1]{3,2,1,0:T(8,128)S(1)}, u32[]{:S(2)}, u32[]{:S(2)}) collective-permute-start(f32[1,16,10,1]{3,2,1,0:T(8,128)S(1)} %get-tuple-element.25), channel_id=1, source_target_pairs={{1,0},{2,1},{3,2},{4,3},{5,4},{6,5},{7,6},{8,7},{9,8},{10,9},{11,1... | collective-permute-start | bytes 1928 | tf_op jit(solution)/shard_map/ppermute | solution.py:22
where the time goes:
time: 345 us; the launch traced here: 344 us
  blocking collectives  221 us (64%)
  starting transfers between devices  59.4 us (17%)
  waiting for transfers between devices  49.3 us (14%)
  other arithmetic  5.19 us (2%)
  between operations  5.09 us (1%)
  local copies, waits for them, and re-layouts  4.04 us (1%)
    psum x2, blocking collectives, energy(): return lax.psum(local_dot(residual, precond), ('gx', 'gy'))  148 us
    psum x1, blocking collectives, local(): curvature = lax.psum(local_dot(direction, image_field), ('gx', 'gy'))  72.9 us
    ppermute x10, waiting for transfers between devices, padded_2(): after = lax.ppermute(first, axis, down)  46.5 us
    ppermute x10, starting transfers between devices, padded_2(): before = lax.ppermute(last, axis, up)  36.2 us
    ppermute x10, starting transfers between devices, padded_2(): after = lax.ppermute(first, axis, down)  23.2 us
  transfers between devices with their start and end apart: 20, of which 11 were waited for; matrix products, arithmetic and copies ran while one was open for 0% of the time, Pallas kernels for 0%

commit v1 on v0

--- a/solution.py
+++ b/solution.py
@@ -154,7 +154,7 @@
 
 
 def energy(residual, precond):
-    return lax.psum(local_dot(residual, precond), ("gx", "gy"))
+    return jnp.sum(lax.all_gather(local_dot(residual, precond), ("gx", "gy")), axis=0)
 
 
 def local(permeability, saturation, pressure_old, source):

time: 345 us -> 347 us (level)
    psum x2 -> x0, blocking collectives: 148 us -> none  [energy(): return lax.psum(local_dot(residual, precond), ('gx', 'gy'))]
    unnamed x0 -> x2, blocking collectives: none -> 148 us
where the time goes in v1:
time: 347 us; the launch traced here: 346 us
  blocking collectives  220 us (63%)
  starting transfers between devices  59.4 us (17%)
  waiting for transfers between devices  49.3 us (14%)
  other arithmetic  6.4 us (2%)
  local copies, waits for them, and re-layouts  5.54 us (2%)
  between operations  5.12 us (1%)
    unnamed x2, blocking collectives  148 us
    psum x1, blocking collectives, local(): curvature = lax.psum(local_dot(direction, image_field), ('gx', 'gy'))  72.9 us
    ppermute x10, waiting for transfers between devices, padded_2(): after = lax.ppermute(first, axis, down)  46.5 us
    ppermute x10, starting transfers between devices, padded_2(): before = lax.ppermute(last, axis, up)  36.2 us
    ppermute x10, starting transfers between devices, padded_2(): after = lax.ppermute(first, axis, down)  23.2 us
  transfers between devices with their start and end apart: 20, of which 11 were waited for; matrix products, arithmetic and copies ran while one was open for 0% of the time, Pallas kernels for 0%

profile of v1, /device:TPU:121, one launch (start us, length us, event | category | flops | bytes accessed | tf_op | source)
XLA Modules:
  0.0 346.2 jit_solution(8314026852423802913)
XLA Ops:
  0.6 0.9 constant_dynamic-update-slice_fusion.2
  1.5 0.8 copy-done.1
  2.4 2.8 collective-permute-start
  5.2 2.5 collective-permute-start.1
  7.7 4.2 %collective-permute-done.1 = f32[3,16,1,128]{3,2,1,0:T(1,128)S(1)} collective-permute-done((f32[3,16,1,128]{3,2,1,0:T(1,128)S(1)}, f32[3,16,1,128]{3,2,1,0:T(1,128)S(1)}, u32[]{:S(2)}, u32[]{:S(2)}) %collective-permute-start.1) | collective-permute-done | bytes 24608 | tf_op jit(solution)/shard_map/ppermute | solution.py:22
  12.1 6.7 %collective-permute-start.2 = (f32[3,16,10,1]{3,2,1,0:T(8,128)S(1)}, f32[3,16,10,1]{3,2,1,0:T(8,128)S(1)}, u32[]{:S(2)}, u32[]{:S(2)}) collective-permute-start(f32[3,16,10,1]{3,2,1,0:T(8,128)S(1)} %get-tuple-element.20), channel_id=1, source_target_pairs={{0,1},{1,2},{2,3},{3,4},{4,5},{5,6},{6,7},{7,8},{8,9},{9,10},{10,1... | collective-permute-start | bytes 5768 | tf_op jit(solution)/shard_map/ppermute | solution.py:21
  18.9 1.9 collective-permute-start.3
  20.8 2.8 collective-permute-done.2
  23.6 5.6 %collective-permute-done.3 = f32[3,16,10,1]{3,2,1,0:T(8,128)S(1)} collective-permute-done((f32[3,16,10,1]{3,2,1,0:T(8,128)S(1)}, f32[3,16,10,1]{3,2,1,0:T(8,128)S(1)}, u32[]{:S(2)}, u32[]{:S(2)}) %collective-permute-start.3) | collective-permute-done | bytes 1952 | tf_op jit(solution)/shard_map/ppermute | solution.py:22
  29.2 0.2 multiply_divide_fusion
  29.6 0.7 copy-done.4
  30.4 0.3 fusion.15
  30.8 0.7 copy-done.2
  31.6 1.9 collective-permute-start.4
  33.5 3.4 collective-permute-start.5
  37.0 3.0 collective-permute-done.5
  40.2 2.9 collective-permute-start.6
  43.1 1.9 collective-permute-start.7
  45.1 5.5 %collective-permute-done.7 = f32[1,16,10,1]{3,2,1,0:T(8,128)S(1)} collective-permute-done((f32[1,16,10,1]{3,2,1,0:T(8,128)S(1)}, f32[1,16,10,1]{3,2,1,0:T(8,128)S(1)}, u32[]{:S(2)}, u32[]{:S(2)}) %collective-permute-start.7) | collective-permute-done | bytes 672 | tf_op jit(solution)/shard_map/ppermute | solution.py:22
  50.7 0.7 multiply_reduce_fusion.1
  51.4 0.8 dynamic-update-slice
  52.2 72.2 %all-reduce.10 = (f32[256]{0:T(256)S(1)}, f32[1]{0:T(128)}) all-reduce(f32[256]{0:T(256)S(1)} %dynamic-update-slice, f32[1]{0:T(128)} %bitcast.3), channel_id=1, replica_groups=mesh['gx'=16,'gy'=16] {'gx','gy'}, use_global_device_ids=true, to_apply=%add.8 | all-reduce | flops 257 | bytes 2056
  124.4 0.6 reduce.6
  126.3 0.6 multiply_reduce_fusion
  126.9 0.7 dynamic-update-slice.1
  127.7 75.4 %all-reduce.9 = f32[256]{0:T(256)S(1)} all-reduce(f32[256]{0:T(256)S(1)} %dynamic-update-slice.1), channel_id=1, replica_groups=mesh['gx'=16,'gy'=16] {'gx','gy'}, use_global_device_ids=true, to_apply=%add.9 | all-reduce | flops 256 | bytes 2048
  203.1 0.6 reduce.7
  205.1 3.1 collective-permute-start.8
  208.2 2.2 collective-permute-start.9
  210.4 4.3 %collective-permute-done.9 = f32[1,16,1,128]{3,2,1,0:T(1,128)S(1)} collective-permute-done((f32[1,16,1,128]{3,2,1,0:T(1,128)S(1)}, f32[1,16,1,128]{3,2,1,0:T(1,128)S(1)}, u32[]{:S(2)}, u32[]{:S(2)}) %collective-permute-start.9) | collective-permute-done | bytes 8224 | tf_op jit(solution)/shard_map/ppermute | solution.py:22
  214.8 4.8 %collective-permute-start.10 = (f32[1,16,10,1]{3,2,1,0:T(8,128)S(1)}, f32[1,16,10,1]{3,2,1,0:T(8,128)S(1)}, u32[]{:S(2)}, u32[]{:S(2)}) collective-permute-start(f32[1,16,10,1]{3,2,1,0:T(8,128)S(1)} %get-tuple-element.28), channel_id=1, source_target_pairs={{0,1},{1,2},{2,3},{3,4},{4,5},{5,6},{6,7},{7,8},{8,9},{9,10},{10,1... | collective-permute-start | bytes 1928 | tf_op jit(solution)/shard_map/ppermute | solution.py:21
  219.6 1.9 collective-permute-start.11
  221.6 5.5 %collective-permute-done.11 = f32[1,16,10,1]{3,2,1,0:T(8,128)S(1)} collective-permute-done((f32[1,16,10,1]{3,2,1,0:T(8,128)S(1)}, f32[1,16,10,1]{3,2,1,0:T(8,128)S(1)}, u32[]{:S(2)}, u32[]{:S(2)}) %collective-permute-start.11) | collective-permute-done | bytes 672 | tf_op jit(solution)/shard_map/ppermute | solution.py:22
  227.3 0.7 fusion.53
  228.0 72.9 %psum.15 = f32[1]{0:T(128)} all-reduce(f32[1]{0:T(128)} %bitcast.8), channel_id=1, replica_groups=mesh['gx'=16,'gy'=16] {'gx','gy'}, use_global_device_ids=true, to_apply=%region_7.8 | all-reduce | flops 1 | bytes 8 | tf_op jit(solution)/shard_map/psum | solution.py:179
  302.3 3.1 collective-permute-start.12
  305.4 2.2 collective-permute-start.13
  307.6 4.3 %collective-permute-done.13 = f32[1,16,1,128]{3,2,1,0:T(1,128)S(1)} collective-permute-done((f32[1,16,1,128]{3,2,1,0:T(1,128)S(1)}, f32[1,16,1,128]{3,2,1,0:T(1,128)S(1)}, u32[]{:S(2)}, u32[]{:S(2)}) %collective-permute-start.13) | collective-permute-done | bytes 8224 | tf_op jit(solution)/shard_map/ppermute | solution.py:22
  312.0 6.0 %collective-permute-start.14 = (f32[1,16,10,1]{3,2,1,0:T(8,128)S(1)}, f32[1,16,10,1]{3,2,1,0:T(8,128)S(1)}, u32[]{:S(2)}, u32[]{:S(2)}) collective-permute-start(f32[1,16,10,1]{3,2,1,0:T(8,128)S(1)} %get-tuple-element.26), channel_id=1, source_target_pairs={{0,1},{1,2},{2,3},{3,4},{4,5},{5,6},{6,7},{7,8},{8,9},{9,10},{10,1... | collective-permute-start | bytes 1928 | tf_op jit(solution)/shard_map/ppermute | solution.py:21
  318.0 1.9 collective-permute-start.15
  320.1 5.4 %collective-permute-done.15 = f32[1,16,10,1]{3,2,1,0:T(8,128)S(1)} collective-permute-done((f32[1,16,10,1]{3,2,1,0:T(8,128)S(1)}, f32[1,16,10,1]{3,2,1,0:T(8,128)S(1)}, u32[]{:S(2)}, u32[]{:S(2)}) %collective-permute-start.15) | collective-permute-done | bytes 672 | tf_op jit(solution)/shard_map/ppermute | solution.py:22
  325.8 1.9 collective-permute-start.16
  327.8 3.4 collective-permute-start.17
  331.1 3.1 collective-permute-done.17
  334.4 2.9 collective-permute-start.18
  337.3 1.9 collective-permute-start.19
  339.3 5.6 %collective-permute-done.19 = f32[1,16,10,1]{3,2,1,0:T(8,128)S(1)} collective-permute-done((f32[1,16,10,1]{3,2,1,0:T(8,128)S(1)}, f32[1,16,10,1]{3,2,1,0:T(8,128)S(1)}, u32[]{:S(2)}, u32[]{:S(2)}) %collective-permute-start.19) | collective-permute-done | bytes 672 | tf_op jit(solution)/shard_map/ppermute | solution.py:22
  345.5 0.7 fusion.43
  (58 shorter events, 2.8 us)
Async XLA Ops:
  0.6 0.9 copy-start.3
  1.5 0.8 copy-start.1
  2.4 5.3 %collective-permute-start = (f32[3,16,1,128]{3,2,1,0:T(1,128)S(1)}, f32[3,16,1,128]{3,2,1,0:T(1,128)S(1)}, u32[]{:S(2)}, u32[]{:S(2)}) collective-permute-start(f32[3,16,1,128]{3,2,1,0:T(1,128)S(1)} %get-tuple-element.22), channel_id=1, source_target_pairs={{0,16},{16,32},{32,48},{48,64},{64,80},{80,96},{96,112},{112,128},... | collective-permute-start | bytes 73736 | tf_op jit(solution)/shard_map/ppermute | solution.py:21
  5.2 6.7 %collective-permute-start.1 = (f32[3,16,1,128]{3,2,1,0:T(1,128)S(1)}, f32[3,16,1,128]{3,2,1,0:T(1,128)S(1)}, u32[]{:S(2)}, u32[]{:S(2)}) collective-permute-start(f32[3,16,1,128]{3,2,1,0:T(1,128)S(1)} %get-tuple-element.23), channel_id=1, source_target_pairs={{16,0},{32,16},{48,32},{64,48},{80,64},{96,80},{112,96},{128,112},... | collective-permute-start | bytes 73736 | tf_op jit(solution)/shard_map/ppermute | solution.py:22
  12.1 11.5 %collective-permute-start.2 = (f32[3,16,10,1]{3,2,1,0:T(8,128)S(1)}, f32[3,16,10,1]{3,2,1,0:T(8,128)S(1)}, u32[]{:S(2)}, u32[]{:S(2)}) collective-permute-start(f32[3,16,10,1]{3,2,1,0:T(8,128)S(1)} %get-tuple-element.20), channel_id=1, source_target_pairs={{0,1},{1,2},{2,3},{3,4},{4,5},{5,6},{6,7},{7,8},{8,9},{9,10},{10,1... | collective-permute-start | bytes 5768 | tf_op jit(solution)/shard_map/ppermute | solution.py:21
  18.9 10.3 %collective-permute-start.3 = (f32[3,16,10,1]{3,2,1,0:T(8,128)S(1)}, f32[3,16,10,1]{3,2,1,0:T(8,128)S(1)}, u32[]{:S(2)}, u32[]{:S(2)}) collective-permute-start(f32[3,16,10,1]{3,2,1,0:T(8,128)S(1)} %get-tuple-element.21), channel_id=1, source_target_pairs={{1,0},{2,1},{3,2},{4,3},{5,4},{6,5},{7,6},{8,7},{9,8},{10,9},{11,1... | collective-permute-start | bytes 5768 | tf_op jit(solution)/shard_map/ppermute | solution.py:22
  29.5 0.8 copy-start.4
  30.6 0.8 copy-start.2
  31.6 5.4 %collective-permute-start.4 = (f32[1,16,1,128]{3,2,1,0:T(1,128)S(1)}, f32[1,16,1,128]{3,2,1,0:T(1,128)S(1)}, u32[]{:S(2)}, u32[]{:S(2)}) collective-permute-start(f32[1,16,1,128]{3,2,1,0:T(1,128)S(1)} %get-tuple-element.38), channel_id=1, source_target_pairs={{0,16},{16,32},{32,48},{48,64},{64,80},{80,96},{96,112},{112,128},... | collective-permute-start | bytes 24584 | tf_op jit(solution)/shard_map/ppermute | solution.py:21
  33.5 6.5 %collective-permute-start.5 = (f32[1,16,1,128]{3,2,1,0:T(1,128)S(1)}, f32[1,16,1,128]{3,2,1,0:T(1,128)S(1)}, u32[]{:S(2)}, u32[]{:S(2)}) collective-permute-start(f32[1,16,1,128]{3,2,1,0:T(1,128)S(1)} %get-tuple-element.39), channel_id=1, source_target_pairs={{16,0},{32,16},{48,32},{64,48},{80,64},{96,80},{112,96},{128,112},... | collective-permute-start | bytes 24584 | tf_op jit(solution)/shard_map/ppermute | solution.py:22
  40.2 4.9 %collective-permute-start.6 = (f32[1,16,10,1]{3,2,1,0:T(8,128)S(1)}, f32[1,16,10,1]{3,2,1,0:T(8,128)S(1)}, u32[]{:S(2)}, u32[]{:S(2)}) collective-permute-start(f32[1,16,10,1]{3,2,1,0:T(8,128)S(1)} %get-tuple-element.30), channel_id=1, source_target_pairs={{0,1},{1,2},{2,3},{3,4},{4,5},{5,6},{6,7},{7,8},{8,9},{9,10},{10,1... | collective-permute-start | bytes 1928 | tf_op jit(solution)/shard_map/ppermute | solution.py:21
  43.1 7.5 %collective-permute-start.7 = (f32[1,16,10,1]{3,2,1,0:T(8,128)S(1)}, f32[1,16,10,1]{3,2,1,0:T(8,128)S(1)}, u32[]{:S(2)}, u32[]{:S(2)}) collective-permute-start(f32[1,16,10,1]{3,2,1,0:T(8,128)S(1)} %get-tuple-element.31), channel_id=1, source_target_pairs={{1,0},{2,1},{3,2},{4,3},{5,4},{6,5},{7,6},{8,7},{9,8},{10,9},{11,1... | collective-permute-start | bytes 1928 | tf_op jit(solution)/shard_map/ppermute | solution.py:22
  205.1 5.3 %collective-permute-start.8 = (f32[1,16,1,128]{3,2,1,0:T(1,128)S(1)}, f32[1,16,1,128]{3,2,1,0:T(1,128)S(1)}, u32[]{:S(2)}, u32[]{:S(2)}) collective-permute-start(f32[1,16,1,128]{3,2,1,0:T(1,128)S(1)} %get-tuple-element.36), channel_id=1, source_target_pairs={{0,16},{16,32},{32,48},{48,64},{64,80},{80,96},{96,112},{112,128},... | collective-permute-start | bytes 24584 | tf_op jit(solution)/shard_map/ppermute | solution.py:21
  208.2 6.5 %collective-permute-start.9 = (f32[1,16,1,128]{3,2,1,0:T(1,128)S(1)}, f32[1,16,1,128]{3,2,1,0:T(1,128)S(1)}, u32[]{:S(2)}, u32[]{:S(2)}) collective-permute-start(f32[1,16,1,128]{3,2,1,0:T(1,128)S(1)} %get-tuple-element.37), channel_id=1, source_target_pairs={{16,0},{32,16},{48,32},{64,48},{80,64},{96,80},{112,96},{128,112},... | collective-permute-start | bytes 24584 | tf_op jit(solution)/shard_map/ppermute | solution.py:22
  214.8 6.8 %collective-permute-start.10 = (f32[1,16,10,1]{3,2,1,0:T(8,128)S(1)}, f32[1,16,10,1]{3,2,1,0:T(8,128)S(1)}, u32[]{:S(2)}, u32[]{:S(2)}) collective-permute-start(f32[1,16,10,1]{3,2,1,0:T(8,128)S(1)} %get-tuple-element.28), channel_id=1, source_target_pairs={{0,1},{1,2},{2,3},{3,4},{4,5},{5,6},{6,7},{7,8},{8,9},{9,10},{10,1... | collective-permute-start | bytes 1928 | tf_op jit(solution)/shard_map/ppermute | solution.py:21
  219.6 7.5 %collective-permute-start.11 = (f32[1,16,10,1]{3,2,1,0:T(8,128)S(1)}, f32[1,16,10,1]{3,2,1,0:T(8,128)S(1)}, u32[]{:S(2)}, u32[]{:S(2)}) collective-permute-start(f32[1,16,10,1]{3,2,1,0:T(8,128)S(1)} %get-tuple-element.29), channel_id=1, source_target_pairs={{1,0},{2,1},{3,2},{4,3},{5,4},{6,5},{7,6},{8,7},{9,8},{10,9},{11,1... | collective-permute-start | bytes 1928 | tf_op jit(solution)/shard_map/ppermute | solution.py:22
  302.2 43.1 %copy-start = (f32[1,16,8,128]{3,2,1,0:T(8,128)}, f32[1,16,8,128]{3,2,1,0:T(8,128)S(1)}, u32[]{:S(2)}) copy-start(f32[1,16,8,128]{3,2,1,0:T(8,128)S(1)} %multiply_add_fusion.1) | copy-start | bytes 196612
  302.3 5.3 %collective-permute-start.12 = (f32[1,16,1,128]{3,2,1,0:T(1,128)S(1)}, f32[1,16,1,128]{3,2,1,0:T(1,128)S(1)}, u32[]{:S(2)}, u32[]{:S(2)}) collective-permute-start(f32[1,16,1,128]{3,2,1,0:T(1,128)S(1)} %get-tuple-element.34), channel_id=1, source_target_pairs={{0,16},{16,32},{32,48},{48,64},{64,80},{80,96},{96,112},{112,128},... | collective-permute-start | bytes 24584 | tf_op jit(solution)/shard_map/ppermute | solution.py:21
  305.4 6.5 %collective-permute-start.13 = (f32[1,16,1,128]{3,2,1,0:T(1,128)S(1)}, f32[1,16,1,128]{3,2,1,0:T(1,128)S(1)}, u32[]{:S(2)}, u32[]{:S(2)}) collective-permute-start(f32[1,16,1,128]{3,2,1,0:T(1,128)S(1)} %get-tuple-element.35), channel_id=1, source_target_pairs={{16,0},{32,16},{48,32},{64,48},{80,64},{96,80},{112,96},{128,112},... | collective-permute-start | bytes 24584 | tf_op jit(solution)/shard_map/ppermute | solution.py:22
  312.0 8.1 %collective-permute-start.14 = (f32[1,16,10,1]{3,2,1,0:T(8,128)S(1)}, f32[1,16,10,1]{3,2,1,0:T(8,128)S(1)}, u32[]{:S(2)}, u32[]{:S(2)}) collective-permute-start(f32[1,16,10,1]{3,2,1,0:T(8,128)S(1)} %get-tuple-element.26), channel_id=1, source_target_pairs={{0,1},{1,2},{2,3},{3,4},{4,5},{5,6},{6,7},{7,8},{8,9},{9,10},{10,1... | collective-permute-start | bytes 1928 | tf_op jit(solution)/shard_map/ppermute | solution.py:21
  318.0 7.5 %collective-permute-start.15 = (f32[1,16,10,1]{3,2,1,0:T(8,128)S(1)}, f32[1,16,10,1]{3,2,1,0:T(8,128)S(1)}, u32[]{:S(2)}, u32[]{:S(2)}) collective-permute-start(f32[1,16,10,1]{3,2,1,0:T(8,128)S(1)} %get-tuple-element.27), channel_id=1, source_target_pairs={{1,0},{2,1},{3,2},{4,3},{5,4},{6,5},{7,6},{8,7},{9,8},{10,9},{11,1... | collective-permute-start | bytes 1928 | tf_op jit(solution)/shard_map/ppermute | solution.py:22
  325.8 5.3 %collective-permute-start.16 = (f32[1,16,1,128]{3,2,1,0:T(1,128)S(1)}, f32[1,16,1,128]{3,2,1,0:T(1,128)S(1)}, u32[]{:S(2)}, u32[]{:S(2)}) collective-permute-start(f32[1,16,1,128]{3,2,1,0:T(1,128)S(1)} %get-tuple-element.32), channel_id=1, source_target_pairs={{0,16},{16,32},{32,48},{48,64},{64,80},{80,96},{96,112},{112,128},... | collective-permute-start | bytes 24584 | tf_op jit(solution)/shard_map/ppermute | solution.py:21
  327.8 6.5 %collective-permute-start.17 = (f32[1,16,1,128]{3,2,1,0:T(1,128)S(1)}, f32[1,16,1,128]{3,2,1,0:T(1,128)S(1)}, u32[]{:S(2)}, u32[]{:S(2)}) collective-permute-start(f32[1,16,1,128]{3,2,1,0:T(1,128)S(1)} %get-tuple-element.33), channel_id=1, source_target_pairs={{16,0},{32,16},{48,32},{64,48},{80,64},{96,80},{112,96},{128,112},... | collective-permute-start | bytes 24584 | tf_op jit(solution)/shard_map/ppermute | solution.py:22
  334.4 4.9 %collective-permute-start.18 = (f32[1,16,10,1]{3,2,1,0:T(8,128)S(1)}, f32[1,16,10,1]{3,2,1,0:T(8,128)S(1)}, u32[]{:S(2)}, u32[]{:S(2)}) collective-permute-start(f32[1,16,10,1]{3,2,1,0:T(8,128)S(1)} %get-tuple-element.24), channel_id=1, source_target_pairs={{0,1},{1,2},{2,3},{3,4},{4,5},{5,6},{6,7},{7,8},{8,9},{9,10},{10,1... | collective-permute-start | bytes 1928 | tf_op jit(solution)/shard_map/ppermute | solution.py:21
  337.3 7.5 %collective-permute-start.19 = (f32[1,16,10,1]{3,2,1,0:T(8,128)S(1)}, f32[1,16,10,1]{3,2,1,0:T(8,128)S(1)}, u32[]{:S(2)}, u32[]{:S(2)}) collective-permute-start(f32[1,16,10,1]{3,2,1,0:T(8,128)S(1)} %get-tuple-element.25), channel_id=1, source_target_pairs={{1,0},{2,1},{3,2},{4,3},{5,4},{6,5},{7,6},{8,7},{9,8},{10,9},{11,1... | collective-permute-start | bytes 1928 | tf_op jit(solution)/shard_map/ppermute | solution.py:22
